TPU v7x, 32 devices: a whole 2x2x4 slice. The times are simulated.
32 devices in a mesh: groups: 2 (over y), ctx: 4 (over z), wt: 2 (over x), sub: 2 (over core).
Axes of the slice: x: 2, y: 2, z: 4, core: 2. Of those that a mesh axis runs over, the one named last changes fastest.
Arguments:
- queries: bfloat16 [16, 32, 128, 576], P(('groups', 'ctx'), None, ('wt', 'sub')), parts along dimension 0, may hold values from -80 to 80
- selection: int32 [16, 4, 2], P(('groups', 'ctx')), parts along dimension 0, may hold values from -1 to 15, as said below
- latent_cache: bfloat16 [128, 64, 576], P(('groups', 'ctx')), parts along dimension 0, may hold values from -8 to 8
- value_up: bfloat16 [128, 512, 128], P(None, ('wt', 'sub')), may hold values from -1 to 1
Outputs:
- attended: bfloat16 [16, 32, 128, 128], P(('groups', 'ctx'), None, ('wt', 'sub')), parts along dimension 0
There are 2 independent parts, one for each index of `groups`. A program takes and returns all parts, laid end to end along the dimension named above; an argument that names none is the same for every part. Nothing has to cross between parts.
Inputs may be any that keep to these rules, and one draw needn't show every extreme that they name: `selection`: entry [c, o, s] is the number of a block among the 16 of owner o, or -1 for an empty slot; in an owner's slots live entries come first and differ. Each query block has 4 live entries in all, and in every query block some owner fills all 2 slots.
All inputs are finite; a program needn't handle non-finite values.
Results may differ from a plain program's by a relative error of at most 0.008.
Values may be sent and summed in bfloat16 or wider, within the bound.
No kernel may reach another device: no remote copies, remote signals or barrier semaphores. Data moves between devices by JAX's collectives and lax.ppermute only.
A program may use at most 128 MiB of HBM per device.

v0:
```python
import jax
import jax.numpy as jnp
from jax import lax
from jax.experimental import pallas as pl
from jax.experimental.pallas import tpu as pltpu
from jax.sharding import PartitionSpec as P

LAT = 512
ROPE = 64
NOPE = 128
SCALE = (NOPE + ROPE) ** (-0.5)
AXES = ("groups", "ctx", "wt", "sub")
PARTS = (9, 11)


SMEM = pl.BlockSpec(memory_space=pltpu.SMEM)
VMEM = pl.BlockSpec(memory_space=pltpu.VMEM)
ANY = pl.BlockSpec(memory_space=pl.ANY)
HBM = pl.BlockSpec(memory_space=pltpu.HBM)


def hop(array, move, **names):
    axes = tuple(name for name in AXES if name in names)
    sizes = [names[name] for name in axes]
    total = 1
    for size in sizes:
        total *= size
    pairs = []
    for at in range(total):
        left, place = at, []
        for size in reversed(sizes):
            place.insert(0, left % size)
            left //= size
        flat = 0
        for size, index in zip(sizes, move(*place)):
            flat = flat * size + index
        pairs.append((at, flat))
    return lax.ppermute(array, axes, pairs)


def pick(asked, cache, spans):
    parts = len(asked)
    block, width = cache.shape[1:]
    whole = asked[0].shape[0] > spans

    def kernel(*refs):
        asked_refs, cache_ref, out_refs = refs[:parts], refs[parts], refs[parts + 1 :]
        mine, slot = lax.axis_index("ctx"), lax.axis_index("sub")
        for part in range(parts):
            for first in range(0, asked[part].shape[0], spans):
                out = out_refs[0].at[first // spans] if whole else out_refs[part]
                tails = []
                for span in range(spans):
                    number = jnp.maximum(asked_refs[part][first + span, slot, mine], 0)
                    out[:, span * LAT : (span + 1) * LAT] = cache_ref[number, :, :LAT]
                    tails.append(cache_ref[number, :, LAT:])
                out[:, spans * LAT :] = jnp.concatenate(tails, axis=1)

    shape = (block, spans * width)
    if whole:
        shapes = [jax.ShapeDtypeStruct((asked[0].shape[0] // spans,) + shape, cache.dtype)]
    else:
        shapes = [jax.ShapeDtypeStruct(shape, cache.dtype)] * parts
    return pl.pallas_call(
        kernel,
        out_shape=shapes,
        in_specs=[SMEM] * parts + [VMEM],
        out_specs=[VMEM] * len(shapes),
        compiler_params=pltpu.CompilerParams(vmem_limit_bytes=16 << 20),
        name="pick",
    )(*asked, cache)


def cut(value_up, wanted):
    count = sum(len(runs) for runs in wanted)

    def kernel(whole_ref, *refs):
        outs, sems = refs[:-1], refs[-1]
        place = [lax.axis_index(name) for name in AXES]
        copies = []
        for runs, out in zip(wanted, outs):
            at = 0
            for first, heads in runs:
                copies.append(
                    pltpu.make_async_copy(
                        whole_ref.at[pl.ds(first(*place), heads)],
                        out.at[pl.ds(at, heads)],
                        sems.at[len(copies)],
                    )
                )
                at += heads
        for copy in copies:
            copy.start()
        for copy in copies:
            copy.wait()

    return pl.pallas_call(
        kernel,
        out_shape=[
            jax.ShapeDtypeStruct(
                (sum(heads for _, heads in runs),) + value_up.shape[1:], value_up.dtype
            )
            for runs in wanted
        ],
        in_specs=[HBM],
        out_specs=[VMEM] * len(wanted),
        scratch_shapes=[pltpu.SemaphoreType.DMA((count,))],
        compiler_params=pltpu.CompilerParams(vmem_limit_bytes=16 << 20),
        name="cut",
    )(pltpu.with_memory_space_constraint(value_up, pltpu.HBM))


def weight_pieces(value_up, heads, query):
    groups, ctx, wide, subs = (lax.axis_size(name) for name in AXES)
    pieces = [value_up]
    rules = [lambda g, c, w, s: [((w * subs + s) * heads, w * subs + s, 0, heads)]]
    square = groups == 2 and subs == 2 and ctx % 2 == 0
    one, two = heads * PARTS[0] // 32, heads * PARTS[1] // 32
    last = 2 * one + two
    rest = heads - last
    sizes = dict(groups=groups, wt=wide, sub=subs)
    wanted, labels, moves = [], [], []

    def want(label, step, core, runs, move):
        def first_of(start):
            return lambda g, c, w, s: ((w + step) % wide * subs + core(g, s)) * heads + start(c)

        wanted.append([(first_of(start), count) for start, count in runs])
        labels.append(label)
        moves.append(move)

    for step in range(1, wide):
        if square:
            same = lambda g, w, s, step=step: (g, (w + step) % wide, s ^ g)
            cross = lambda g, w, s, step=step: (g, (w + step) % wide, s ^ g ^ 1)
            here, there = lambda g, s: s ^ g, lambda g, s: s ^ g ^ 1
            want("wone", step, here, [(lambda c: c % 2 * one, one)], same)
            want("wtwo", step, here, [(lambda c: 2 * one, two)], same)
            want("wsame", step, here, [(lambda c: last, rest)], same)
            want(
                "wcross",
                step,
                there,
                [(lambda c: (1 - c % 2) * one, one), (lambda c: last, rest)],
                cross,
            )
        else:
            for twist in range(subs):
                move = lambda g, w, s, step=step, twist=twist: (
                    g,
                    (w + step) % wide,
                    (s + twist) % subs,
                )
                there = lambda g, s, twist=twist: (s + twist) % subs
                want("wfar", step, there, [(lambda c: 0, heads)], move)
    for step in range(1, subs):
        there = lambda g, s, step=step: (s + step) % subs
        move = lambda g, w, s, step=step: (g, w, (s + step) % subs)
        want("wcore", 0, there, [(lambda c: 0, heads)], move)
    got = [None] * len(wanted)
    ahead = [at for at, label in enumerate(labels) if label == "wone"]
    for chosen in (ahead, [at for at in range(len(labels)) if at not in ahead]):
        if not chosen:
            continue
        found = cut(value_up, [wanted[at] for at in chosen])
        for at, piece in zip(chosen, found):
            got[at] = hop(piece, moves[at], **sizes)

    def add(piece, step, core, runs):
        pieces.append(piece)

        def rule(g, c, w, s):
            at, found = 0, []
            for start, count in runs:
                found.append((at, (w - step) % wide * subs + core(g, s), start(c), count))
                at += count
            return found

        rules.append(rule)

    at = 0
    for step in range(1, wide):
        if square:
            first, second, direct, crossed = got[at : at + 4]
            at += 4
            swap = lambda g: (g ^ 1,)
            side_first = hop(first, swap, groups=groups)
            over = hop(first, lambda c: (c ^ 1,), ctx=ctx)
            second, query = lax.optimization_barrier((second, query))
            side_second = hop(second, swap, groups=groups)
            here, there = lambda g, s: s ^ g, lambda g, s: s ^ g ^ 1
            own, next_to = lambda c: c % 2 * one, lambda c: (1 - c % 2) * one
            add(first, step, here, [(own, one)])
            add(over, step, here, [(next_to, one)])
            add(second, step, here, [(lambda c: 2 * one, two)])
            add(direct, step, here, [(lambda c: last, rest)])
            add(side_first, step, there, [(own, one)])
            add(side_second, step, there, [(lambda c: 2 * one, two)])
            add(crossed, step, there, [(next_to, one), (lambda c: last, rest)])
        else:
            for twist in range(subs):
                there = lambda g, s, twist=twist: (s - twist) % subs
                add(got[at], step, there, [(lambda c: 0, heads)])
                at += 1
    for step in range(1, subs):
        add(got[at], 0, lambda g, s, step=step: (s - step) % subs, [(lambda c: 0, heads)])
        at += 1
    return pieces, rules, query, 2 * one if square else 0


def attend(selection, query, mine, other, mixed):
    spans, heads, per_span, width = query.shape
    _, slots, owners = selection.shape
    block = mine[0].shape[-2]
    rotary = width - LAT
    chunks = 2
    group = heads // chunks
    landed = len(mine)

    def kernel(chosen_ref, query_ref, *refs):
        mine_refs, other_refs = refs[:landed], refs[landed : 2 * landed]
        latent, keys = refs[2 * landed :]
        at, sub = lax.axis_index("ctx"), lax.axis_index("sub")
        for span in range(spans):
            filled = jnp.int32(0)
            latent_at = slice(span * LAT, (span + 1) * LAT)
            for entry in range(owners):
                owner = at ^ entry if mixed else entry
                own = mine_refs[entry] if mixed else mine_refs[0].at[entry]
                across = other_refs[entry] if mixed else other_refs[0].at[entry]
                for slot in range(slots):
                    live = chosen_ref[span, slot, owner] >= 0
                    here = sub == slot
                    start = pl.multiple_of(jnp.minimum(filled, owners - 1) * block, block)

                    @pl.when(live)
                    def _():
                        keys[span, pl.ds(start, block), :LAT] = jnp.where(
                            here, own[:, latent_at], across[:, latent_at]
                        )
                        keys[span, pl.ds(start, block), LAT:] = jnp.where(
                            here, own[:, spans * LAT :], across[:, spans * LAT :]
                        )

                    filled = filled + live.astype(jnp.int32)
            if span:
                at_span = LAT + span * rotary
                keys[span, :, LAT:width] = keys[span, :, at_span : at_span + rotary]

        def score(step):
            span, first = step % spans, step // spans * group
            lines = query_ref[span, first : first + group].reshape(group * per_span, width)
            return lax.dot_general(
                lines,
                keys[span, :, :width],
                (((1,), (1,)), ((), ())),
                preferred_element_type=jnp.float32,
            )

        def soften(scores):
            top = jnp.max(scores, axis=1, keepdims=True)
            expo = jnp.exp((scores - top) * jnp.float32(SCALE))
            return expo.astype(jnp.bfloat16), 1.0 / jnp.sum(expo, axis=1, keepdims=True)

        def gather(step, expo, inverse):
            span, first = step % spans, step // spans * group
            mixed_rows = jnp.dot(expo, keys[span, :, :LAT], preferred_element_type=jnp.float32)
            latent[first : first + group, span] = (
                (mixed_rows * inverse).astype(jnp.bfloat16).reshape(group, per_span, LAT)
            )

        steps = chunks * spans
        scores = {step: score(step) for step in range(min(2, steps))}
        soft = {0: soften(scores.pop(0))}
        for step in range(steps):
            if step + 2 < steps:
                scores[step + 2] = score(step + 2)
            if step + 1 < steps:
                soft[step + 1] = soften(scores.pop(step + 1))
            gather(step, *soft.pop(step))

    return pl.pallas_call(
        kernel,
        out_shape=jax.ShapeDtypeStruct((heads, spans, per_span, LAT), jnp.bfloat16),
        in_specs=[SMEM] + [VMEM] * (1 + 2 * landed),
        out_specs=VMEM,
        scratch_shapes=[pltpu.VMEM((spans, owners * block, LAT + spans * rotary), jnp.bfloat16)],
        compiler_params=pltpu.CompilerParams(vmem_limit_bytes=(16 if mixed else 44) << 20),
        name="attend",
    )(selection, query, *mine, *other)


def project(latent, pieces, rules, split):
    heads, spans, per_span, _ = latent.shape
    rows, values = pieces[0].shape[1:]
    tokens = spans * per_span
    parts = len(pieces)
    pitch = heads + 8

    def kernel(latent_ref, *refs):
        piece_refs = refs[:parts]
        out_ref, weights, summed, result, weight_sems, out_sem = refs[parts:]
        place = [lax.axis_index(name) for name in AXES]
        arrivals = [[], []]

        def bring(group, piece, head_from, number, head_to, count):
            row_at = pl.multiple_of(number * rows, rows)
            arrivals[group].append(
                pltpu.make_async_copy(
                    piece.at[pl.ds(head_from, count)],
                    weights.at[pl.ds(head_to, count), pl.ds(row_at, rows)],
                    weight_sems.at[group],
                )
            )

        for piece, rule in zip(piece_refs, rules):
            for head_from, number, head_to, count in rule(*place):
                if not isinstance(head_to, int) or head_to + count <= split:
                    bring(1, piece, head_from, number, head_to, count)
                elif head_to >= split:
                    bring(0, piece, head_from, number, head_to, count)
                else:
                    low = split - head_to
                    bring(0, piece, head_from + low, number, split, count - low)
                    bring(1, piece, head_from, number, head_to, low)
        for group in arrivals:
            for copy in group:
                copy.start()

        departures = []
        done = set()
        for position, head in enumerate(list(range(split, heads)) + list(range(split - 1, -1, -1))):
            if position in (0, heads - split):
                for copy in arrivals[0 if position == 0 and split < heads else 1]:
                    copy.wait()
            summed[pl.ds(head, tokens, stride=pitch), :] = jnp.dot(
                latent_ref[head].reshape(tokens, LAT),
                weights[head],
                preferred_element_type=jnp.float32,
            )
            done.add(head)
            first = head // 16 * 16
            if not done.issuperset(range(first, first + 16)):
                continue
            for token in range(tokens):
                line = summed[token * pitch + first : token * pitch + first + 16, :]
                result[token // per_span, token % per_span, first : first + 16] = line.astype(
                    jnp.bfloat16
                )
            departures.append(
                pltpu.make_async_copy(
                    result.at[:, :, pl.ds(first, 16)], out_ref.at[:, :, pl.ds(first, 16)], out_sem
                )
            )
            departures[-1].start()
        for copy in departures:
            copy.wait()

    return pl.pallas_call(
        kernel,
        out_shape=jax.ShapeDtypeStruct((spans, per_span, heads, values), jnp.bfloat16),
        in_specs=[VMEM, HBM] + [ANY] * (parts - 1),
        out_specs=ANY,
        scratch_shapes=[
            pltpu.VMEM((heads, LAT, values), jnp.bfloat16),
            pltpu.VMEM((tokens * pitch, values), jnp.float32),
            pltpu.VMEM((spans, per_span, heads, values), jnp.bfloat16),
            pltpu.SemaphoreType.DMA((2,)),
            pltpu.SemaphoreType.DMA,
        ],
        compiler_params=pltpu.CompilerParams(vmem_limit_bytes=16 << 20),
        name="project",
    )(latent, *pieces)


def per_device(queries, selection, latent_cache, value_up):
    owners, subs = lax.axis_size("ctx"), lax.axis_size("sub")
    spans, _, heads, _ = queries.shape
    chosen = jnp.transpose(selection, (0, 2, 1))
    mixed = owners <= 8

    if mixed:
        asked = [chosen] * owners
        order = sorted(range(1, owners), key=lambda e: (e == 1, e))
        for entry in order:
            asked[entry] = hop(chosen, lambda c: (c ^ entry,), ctx=owners)
        picked = pick(asked, latent_cache, spans)
        mine = [picked[0]]
        for entry in range(1, owners):
            mine.append(hop(picked[entry], lambda c: (c ^ entry,), ctx=owners))
    else:
        asked = [lax.all_gather(chosen, "ctx", axis=0, tiled=True)]
        found = pick(asked, latent_cache, spans)[0]
        mine = [lax.all_to_all(found, "ctx", split_axis=0, concat_axis=0, tiled=True)]
    other = []
    for entry, piece in enumerate(mine):
        other.append(hop(piece, lambda s: (s ^ 1,), sub=subs))
    query = jnp.transpose(queries, (0, 2, 1, 3))
    pieces, rules, query, split = weight_pieces(value_up, heads, query)
    latent = attend(chosen, query, mine, other, mixed)
    return project(latent, pieces, rules, split)


def solution(mesh):
    placed = (
        P(("groups", "ctx"), None, ("wt", "sub"), None),
        P(("groups", "ctx"), None, None),
        P(("groups", "ctx"), None, None),
        P(None, ("wt", "sub"), None),
    )

    return jax.shard_map(
        per_device,
        mesh=mesh,
        in_specs=placed,
        out_specs=P(("groups", "ctx"), None, ("wt", "sub"), None),
        check_vma=False,
    )
```

profile of v0, /device:TPU:0, one launch (start us, length us, event | category | flops | bytes accessed | tf_op | source)
XLA Modules:
  0.0 52.8 jit_solution(7769442727063598675)
XLA Ops:
  0.0 1.6 %cut.2 = (bf16[11,128,128]{2,1,0:T(8,128)(2,1)S(1)}, bf16[3,128,128]{2,1,0:T(8,128)(2,1)S(1)}, bf16[12,128,128]{2,1,0:T(8,128)(2,1)S(1)}, bf16[32,128,128]{2,1,0:T(8,128)(2,1)S(1)}) custom-call(bf16[128,128,128]{2,1,0:T(8,128)(2,1)} %refs_0_.1), custom_call_target="tpu_custom_call" | custom-call | tf_op jit(solution)/shard_map/cut/pallas_call | solution.py:97
  1.7 0.6 %collective-permute-start.17 = (bf16[32,128,128]{2,1,0:T(8,128)(2,1)S(1)}, bf16[32,128,128]{2,1,0:T(8,128)(2,1)S(1)}, u32[]{:S(2)}, u32[]{:S(2)}) collective-permute-start(bf16[32,128,128]{2,1,0:T(8,128)(2,1)S(1)} %get-tuple-element.24), channel_id=1, source_target_pairs={{0,1},{1,0},{2,3},{3,2},{16,17},{17,16},{18,19},{19,18},{4,5},{5,4... | collective-permute-start | bytes 3145736 | tf_op jit(solution)/shard_map/ppermute | solution.py:38
  2.2 2.6 %collective-permute-start.13 = (bf16[3,128,128]{2,1,0:T(8,128)(2,1)S(1)}, bf16[3,128,128]{2,1,0:T(8,128)(2,1)S(1)}, u32[]{:S(2)}, u32[]{:S(2)}) collective-permute-start(bf16[3,128,128]{2,1,0:T(8,128)(2,1)S(1)} %get-tuple-element.22), channel_id=1, source_target_pairs={{0,2},{1,3},{2,0},{3,1},{16,19},{17,18},{18,17},{19,16},{4,6},{5,7... | collective-permute-start | bytes 294920 | tf_op jit(solution)/shard_map/ppermute | solution.py:38
  4.8 1.6 %collective-permute-start.1 = (s32[2,2,4]{2,1,0:T(2,128)S(1)}, s32[2,2,4]{2,1,0:T(2,128)S(1)}, u32[]{:S(2)}, u32[]{:S(2)}) collective-permute-start(s32[2,2,4]{2,1,0:T(2,128)S(1)} %bitcast.5), channel_id=1, source_target_pairs={{0,4},{4,0},{8,12},{12,8},{1,5},{5,1},{9,13},{13,9},{2,6},{6,2},{1... | collective-permute-start | bytes 200 | tf_op jit(solution)/shard_map/ppermute | solution.py:38
  6.4 2.6 %collective-permute-start.2 = (s32[2,2,4]{2,1,0:T(2,128)S(1)}, s32[2,2,4]{2,1,0:T(2,128)S(1)}, u32[]{:S(2)}, u32[]{:S(2)}) collective-permute-start(s32[2,2,4]{2,1,0:T(2,128)S(1)} %bitcast.6), channel_id=1, source_target_pairs={{0,8},{4,12},{8,0},{12,4},{1,9},{5,13},{9,1},{13,5},{2,10},{6,14},... | collective-permute-start | bytes 200 | tf_op jit(solution)/shard_map/ppermute | solution.py:38
  8.9 0.2 collective-permute-start.3
  9.2 1.7 %collective-permute-done.2.refs_2_ = s32[2,2,4]{2,1,0:T(2,128)S(1)} collective-permute-done((s32[2,2,4]{2,1,0:T(2,128)S(1)}, s32[2,2,4]{2,1,0:T(2,128)S(1)}, u32[]{:S(2)}, u32[]{:S(2)}) %collective-permute-start.2) | collective-permute-done | bytes 96 | tf_op jit(solution)/shard_map/ppermute | solution.py:38
  10.8 3.6 %collective-permute-done.3.refs_3_ = s32[2,2,4]{2,1,0:T(2,128)S(1)} collective-permute-done((s32[2,2,4]{2,1,0:T(2,128)S(1)}, s32[2,2,4]{2,1,0:T(2,128)S(1)}, u32[]{:S(2)}, u32[]{:S(2)}) %collective-permute-start.3) | collective-permute-done | bytes 96 | tf_op jit(solution)/shard_map/ppermute | solution.py:38
  14.4 0.8 %pick.1 = (bf16[64,1152]{1,0:T(8,128)(2,1)S(1)}, bf16[64,1152]{1,0:T(8,128)(2,1)S(1)}, bf16[64,1152]{1,0:T(8,128)(2,1)S(1)}, bf16[64,1152]{1,0:T(8,128)(2,1)S(1)}) custom-call(s32[2,2,4]{2,1,0:T(2,128)S(1)} %bitcast.8, s32[2,2,4]{2,1,0:T(2,128)S(1)} %collective-permute-done.1.refs_1_, s32[2,2,4]{2,1,0:T(2,128)S(1)} %collective-permute-done.2.refs_2_, ...), custom_call_target="tpu_custom_call" | custom-call | tf_op jit(solution)/shard_map/pick/pallas_call | solution.py:64
  15.2 0.2 collective-permute-start.6
  15.4 0.5 collective-permute-start
  15.9 0.0 collective-permute-start.4
  15.9 1.0 %cut.3 = bf16[9,128,128]{2,1,0:T(8,128)(2,1)S(1)} custom-call(bf16[128,128,128]{2,1,0:T(8,128)(2,1)} %refs_0_.1), custom_call_target="tpu_custom_call" | custom-call | tf_op jit(solution)/shard_map/cut/pallas_call | solution.py:97
  16.9 1.6 %collective-permute-start.11 = (bf16[9,128,128]{2,1,0:T(8,128)(2,1)S(1)}, bf16[9,128,128]{2,1,0:T(8,128)(2,1)S(1)}, u32[]{:S(2)}, u32[]{:S(2)}) collective-permute-start(bf16[9,128,128]{2,1,0:T(8,128)(2,1)S(1)} %cut.3), channel_id=1, source_target_pairs={{0,2},{1,3},{2,0},{3,1},{16,19},{17,18},{18,17},{19,16},{4,6},{5,7... | collective-permute-start | bytes 884744 | tf_op jit(solution)/shard_map/ppermute | solution.py:38
  18.5 5.4 %collective-permute-done.6.refs_3_ = bf16[64,1152]{1,0:T(8,128)(2,1)S(1)} collective-permute-done((bf16[64,1152]{1,0:T(8,128)(2,1)S(1)}, bf16[64,1152]{1,0:T(8,128)(2,1)S(1)}, u32[]{:S(2)}, u32[]{:S(2)}) %collective-permute-start.6) | collective-permute-done | bytes 147488 | tf_op jit(solution)/shard_map/ppermute | solution.py:38
  23.9 6.0 %collective-permute-done.5.refs_2_ = bf16[64,1152]{1,0:T(8,128)(2,1)S(1)} collective-permute-done((bf16[64,1152]{1,0:T(8,128)(2,1)S(1)}, bf16[64,1152]{1,0:T(8,128)(2,1)S(1)}, u32[]{:S(2)}, u32[]{:S(2)}) %collective-permute-start.5) | collective-permute-done | bytes 147488 | tf_op jit(solution)/shard_map/ppermute | solution.py:38
  29.9 0.0 collective-permute-start.10
  29.9 0.0 collective-permute-done.7.refs_4_
  29.9 0.5 collective-permute-start.8
  30.4 0.0 collective-permute-done.11.refs_1_
  30.4 0.1 collective-permute-start.9
  30.5 0.0 collective-permute-done.refs_3_
  30.5 0.6 %collective-permute-start.16 = (bf16[12,128,128]{2,1,0:T(8,128)(2,1)S(1)}, bf16[12,128,128]{2,1,0:T(8,128)(2,1)S(1)}, u32[]{:S(2)}, u32[]{:S(2)}) collective-permute-start(bf16[12,128,128]{2,1,0:T(8,128)(2,1)S(1)} %get-tuple-element.23), channel_id=1, source_target_pairs={{0,3},{1,2},{2,1},{3,0},{16,18},{17,19},{18,16},{19,17},{4,7},{5,6... | collective-permute-start | bytes 1179656 | tf_op jit(solution)/shard_map/ppermute | solution.py:38
  31.1 0.9 %copy.7 = bf16[2,32,32,576]{3,1,2,0:T(8,128)(2,1)S(1)} copy(bf16[2,32,32,576]{3,2,1,0:T(8,128)(2,1)S(1)} %copy-done.3) | data formatting | bytes 4718592 | tf_op args[0]
  32.0 0.0 copy-start
  32.0 3.6 %collective-permute-start.15 = (bf16[11,128,128]{2,1,0:T(8,128)(2,1)S(1)}, bf16[11,128,128]{2,1,0:T(8,128)(2,1)S(1)}, u32[]{:S(2)}, u32[]{:S(2)}) collective-permute-start(bf16[11,128,128]{2,1,0:T(8,128)(2,1)S(1)} %collective-permute-done.refs_3_), channel_id=1, source_target_pairs={{0,16},{16,0},{1,17},{17,1},{2,18},{18,2},{3,19},{19,3},{4,20},{20... | collective-permute-start | bytes 1081352 | tf_op jit(solution)/shard_map/ppermute | solution.py:38
  35.6 0.2 collective-permute-start.14
  35.8 2.5 %attend.1.latent_ref = bf16[32,2,32,512]{3,2,1,0:T(8,128)(2,1)S(1)} custom-call(s32[2,2,4]{2,1,0:T(2,128)S(1)} %bitcast.9, bf16[2,32,32,576]{3,2,1,0:T(8,128)(2,1)S(1)} %bitcast.4, bf16[64,1152]{1,0:T(8,128)(2,1)S(1)} %get-tuple-element.17.refs_0_, bf16[64,1152]{1,0:T(8,128)(2,1)S(1)} %collective-permute-done.4.refs_1_, ...), custom_call_target="tpu_custom_call" | custom-call | tf_op jit(solution)/shard_map/attend/pallas_call | solution.py:282
  38.3 3.0 %collective-permute-done.16.refs_7_ = bf16[12,128,128]{2,1,0:T(8,128)(2,1)S(1)} collective-permute-done((bf16[12,128,128]{2,1,0:T(8,128)(2,1)S(1)}, bf16[12,128,128]{2,1,0:T(8,128)(2,1)S(1)}, u32[]{:S(2)}, u32[]{:S(2)}) %collective-permute-start.16) | collective-permute-done | bytes 393248 | tf_op jit(solution)/shard_map/ppermute | solution.py:38
  41.3 3.1 %collective-permute-done.12.refs_2_ = bf16[9,128,128]{2,1,0:T(8,128)(2,1)S(1)} collective-permute-done((bf16[9,128,128]{2,1,0:T(8,128)(2,1)S(1)}, bf16[9,128,128]{2,1,0:T(8,128)(2,1)S(1)}, u32[]{:S(2)}, u32[]{:S(2)}) %collective-permute-start.12) | collective-permute-done | bytes 294944 | tf_op jit(solution)/shard_map/ppermute | solution.py:38
  44.4 6.3 %collective-permute-done.14.refs_5_ = bf16[9,128,128]{2,1,0:T(8,128)(2,1)S(1)} collective-permute-done((bf16[9,128,128]{2,1,0:T(8,128)(2,1)S(1)}, bf16[9,128,128]{2,1,0:T(8,128)(2,1)S(1)}, u32[]{:S(2)}, u32[]{:S(2)}) %collective-permute-start.14) | collective-permute-done | bytes 294944 | tf_op jit(solution)/shard_map/ppermute | solution.py:38
  50.6 2.2 %project.1 = bf16[2,32,32,128]{3,2,1,0:T(8,128)(2,1)} custom-call(bf16[32,2,32,512]{3,2,1,0:T(8,128)(2,1)S(1)} %attend.1.latent_ref, bf16[128,128,128]{2,1,0:T(8,128)(2,1)S(1)} %copy-done, bf16[9,128,128]{2,1,0:T(8,128)(2,1)S(1)} %collective-permute-done.11.refs_1_, bf16[9,128,128]{2,1,0:T(8,128)(2,1)S(1)} %collective-permute-done.12.refs_2_, ...), custom_call_target="tpu_custom_call" | custom-call | tf_op jit(solution)/shard_map/project/pallas_call | solution.py:359
  (18 shorter events, 0.0 us)
Async XLA Ops:
  0.0 4.8 %copy-start.2 = (s32[2,4,2]{1,2,0:T(2,128)S(1)}, s32[2,4,2]{1,2,0:T(2,128)}, u32[]{:S(2)}) copy-start(s32[2,4,2]{1,2,0:T(2,128)} %param.5) | copy-start | bytes 196
  0.0 14.4 %copy-start.1 = (bf16[16,64,576]{2,1,0:T(8,128)(2,1)S(1)}, bf16[16,64,576]{2,1,0:T(8,128)(2,1)}, u32[]{:S(2)}) copy-start(bf16[16,64,576]{2,1,0:T(8,128)(2,1)} %refs_4_.1) | copy-start | bytes 3538948
  1.7 49.0 %collective-permute-start.17 = (bf16[32,128,128]{2,1,0:T(8,128)(2,1)S(1)}, bf16[32,128,128]{2,1,0:T(8,128)(2,1)S(1)}, u32[]{:S(2)}, u32[]{:S(2)}) collective-permute-start(bf16[32,128,128]{2,1,0:T(8,128)(2,1)S(1)} %get-tuple-element.24), channel_id=1, source_target_pairs={{0,1},{1,0},{2,3},{3,2},{16,17},{17,16},{18,19},{19,18},{4,5},{5,4... | collective-permute-start | bytes 3145736 | tf_op jit(solution)/shard_map/ppermute | solution.py:38
  2.2 14.7 %collective-permute-start.13 = (bf16[3,128,128]{2,1,0:T(8,128)(2,1)S(1)}, bf16[3,128,128]{2,1,0:T(8,128)(2,1)S(1)}, u32[]{:S(2)}, u32[]{:S(2)}) collective-permute-start(bf16[3,128,128]{2,1,0:T(8,128)(2,1)S(1)} %get-tuple-element.22), channel_id=1, source_target_pairs={{0,2},{1,3},{2,0},{3,1},{16,19},{17,18},{18,17},{19,16},{4,6},{5,7... | collective-permute-start | bytes 294920 | tf_op jit(solution)/shard_map/ppermute | solution.py:38
  4.8 26.3 %copy-start.3 = (bf16[2,32,32,576]{3,2,1,0:T(8,128)(2,1)S(1)}, bf16[2,32,32,576]{3,2,1,0:T(8,128)(2,1)}, u32[]{:S(2)}) copy-start(bf16[2,32,32,576]{3,2,1,0:T(8,128)(2,1)} %param.4) | copy-start | bytes 7077892
  4.8 4.4 %collective-permute-start.1 = (s32[2,2,4]{2,1,0:T(2,128)S(1)}, s32[2,2,4]{2,1,0:T(2,128)S(1)}, u32[]{:S(2)}, u32[]{:S(2)}) collective-permute-start(s32[2,2,4]{2,1,0:T(2,128)S(1)} %bitcast.5), channel_id=1, source_target_pairs={{0,4},{4,0},{8,12},{12,8},{1,5},{5,1},{9,13},{13,9},{2,6},{6,2},{1... | collective-permute-start | bytes 200 | tf_op jit(solution)/shard_map/ppermute | solution.py:38
  6.4 4.5 %collective-permute-start.2 = (s32[2,2,4]{2,1,0:T(2,128)S(1)}, s32[2,2,4]{2,1,0:T(2,128)S(1)}, u32[]{:S(2)}, u32[]{:S(2)}) collective-permute-start(s32[2,2,4]{2,1,0:T(2,128)S(1)} %bitcast.6), channel_id=1, source_target_pairs={{0,8},{4,12},{8,0},{12,4},{1,9},{5,13},{9,1},{13,5},{2,10},{6,14},... | collective-permute-start | bytes 200 | tf_op jit(solution)/shard_map/ppermute | solution.py:38
  8.9 5.5 %collective-permute-start.3 = (s32[2,2,4]{2,1,0:T(2,128)S(1)}, s32[2,2,4]{2,1,0:T(2,128)S(1)}, u32[]{:S(2)}, u32[]{:S(2)}) collective-permute-start(s32[2,2,4]{2,1,0:T(2,128)S(1)} %bitcast.7), channel_id=1, source_target_pairs={{0,12},{4,8},{8,4},{12,0},{1,13},{5,9},{9,5},{13,1},{2,14},{6,10},... | collective-permute-start | bytes 200 | tf_op jit(solution)/shard_map/ppermute | solution.py:38
  15.2 8.7 %collective-permute-start.6 = (bf16[64,1152]{1,0:T(8,128)(2,1)S(1)}, bf16[64,1152]{1,0:T(8,128)(2,1)S(1)}, u32[]{:S(2)}, u32[]{:S(2)}) collective-permute-start(bf16[64,1152]{1,0:T(8,128)(2,1)S(1)} %get-tuple-element.20), channel_id=1, source_target_pairs={{0,12},{4,8},{8,4},{12,0},{1,13},{5,9},{9,5},{13,1},{2,14},{6,10},... | collective-permute-start | bytes 442376 | tf_op jit(solution)/shard_map/ppermute | solution.py:38
  15.4 15.1 %collective-permute-start = (bf16[11,128,128]{2,1,0:T(8,128)(2,1)S(1)}, bf16[11,128,128]{2,1,0:T(8,128)(2,1)S(1)}, u32[]{:S(2)}, u32[]{:S(2)}) collective-permute-start(bf16[11,128,128]{2,1,0:T(8,128)(2,1)S(1)} %get-tuple-element.15), channel_id=1, source_target_pairs={{0,2},{1,3},{2,0},{3,1},{16,19},{17,18},{18,17},{19,16},{4,6},{5,7... | collective-permute-start | bytes 1081352 | tf_op jit(solution)/shard_map/ppermute | solution.py:38
  15.9 8.0 %collective-permute-start.4 = (bf16[64,1152]{1,0:T(8,128)(2,1)S(1)}, bf16[64,1152]{1,0:T(8,128)(2,1)S(1)}, u32[]{:S(2)}, u32[]{:S(2)}) collective-permute-start(bf16[64,1152]{1,0:T(8,128)(2,1)S(1)} %get-tuple-element.18), channel_id=1, source_target_pairs={{0,4},{4,0},{8,12},{12,8},{1,5},{5,1},{9,13},{13,9},{2,6},{6,2},{1... | collective-permute-start | bytes 442376 | tf_op jit(solution)/shard_map/ppermute | solution.py:38
  16.9 13.6 %collective-permute-start.11 = (bf16[9,128,128]{2,1,0:T(8,128)(2,1)S(1)}, bf16[9,128,128]{2,1,0:T(8,128)(2,1)S(1)}, u32[]{:S(2)}, u32[]{:S(2)}) collective-permute-start(bf16[9,128,128]{2,1,0:T(8,128)(2,1)S(1)} %cut.3), channel_id=1, source_target_pairs={{0,2},{1,3},{2,0},{3,1},{16,19},{17,18},{18,17},{19,16},{4,6},{5,7... | collective-permute-start | bytes 884744 | tf_op jit(solution)/shard_map/ppermute | solution.py:38
  23.9 6.0 %collective-permute-start.5 = (bf16[64,1152]{1,0:T(8,128)(2,1)S(1)}, bf16[64,1152]{1,0:T(8,128)(2,1)S(1)}, u32[]{:S(2)}, u32[]{:S(2)}) collective-permute-start(bf16[64,1152]{1,0:T(8,128)(2,1)S(1)} %get-tuple-element.19), channel_id=1, source_target_pairs={{0,8},{4,12},{8,0},{12,4},{1,9},{5,13},{9,1},{13,5},{2,10},{6,14},... | collective-permute-start | bytes 442376 | tf_op jit(solution)/shard_map/ppermute | solution.py:38
  23.9 6.0 %collective-permute-start.7 = (bf16[64,1152]{1,0:T(8,128)(2,1)S(1)}, bf16[64,1152]{1,0:T(8,128)(2,1)S(1)}, u32[]{:S(2)}, u32[]{:S(2)}) collective-permute-start(bf16[64,1152]{1,0:T(8,128)(2,1)S(1)} %get-tuple-element.17.refs_0_), channel_id=1, source_target_pairs={{0,1},{1,0},{2,3},{3,2},{4,5},{5,4},{6,7},{7,6},{8,9},{9,8},{10,11... | collective-permute-start | bytes 442376 | tf_op jit(solution)/shard_map/ppermute | solution.py:38
  29.9 2.1 %collective-permute-start.10 = (bf16[64,1152]{1,0:T(8,128)(2,1)S(1)}, bf16[64,1152]{1,0:T(8,128)(2,1)S(1)}, u32[]{:S(2)}, u32[]{:S(2)}) collective-permute-start(bf16[64,1152]{1,0:T(8,128)(2,1)S(1)} %collective-permute-done.6.refs_3_), channel_id=1, source_target_pairs={{0,1},{1,0},{2,3},{3,2},{4,5},{5,4},{6,7},{7,6},{8,9},{9,8},{10,11... | collective-permute-start | bytes 442376 | tf_op jit(solution)/shard_map/ppermute | solution.py:38
  29.9 5.7 %collective-permute-start.8 = (bf16[64,1152]{1,0:T(8,128)(2,1)S(1)}, bf16[64,1152]{1,0:T(8,128)(2,1)S(1)}, u32[]{:S(2)}, u32[]{:S(2)}) collective-permute-start(bf16[64,1152]{1,0:T(8,128)(2,1)S(1)} %collective-permute-done.4.refs_1_), channel_id=1, source_target_pairs={{0,1},{1,0},{2,3},{3,2},{4,5},{5,4},{6,7},{7,6},{8,9},{9,8},{10,11... | collective-permute-start | bytes 442376 | tf_op jit(solution)/shard_map/ppermute | solution.py:38
  30.4 5.2 %collective-permute-start.9 = (bf16[64,1152]{1,0:T(8,128)(2,1)S(1)}, bf16[64,1152]{1,0:T(8,128)(2,1)S(1)}, u32[]{:S(2)}, u32[]{:S(2)}) collective-permute-start(bf16[64,1152]{1,0:T(8,128)(2,1)S(1)} %collective-permute-done.5.refs_2_), channel_id=1, source_target_pairs={{0,1},{1,0},{2,3},{3,2},{4,5},{5,4},{6,7},{7,6},{8,9},{9,8},{10,11... | collective-permute-start | bytes 442376 | tf_op jit(solution)/shard_map/ppermute | solution.py:38
  30.5 10.8 %collective-permute-start.16 = (bf16[12,128,128]{2,1,0:T(8,128)(2,1)S(1)}, bf16[12,128,128]{2,1,0:T(8,128)(2,1)S(1)}, u32[]{:S(2)}, u32[]{:S(2)}) collective-permute-start(bf16[12,128,128]{2,1,0:T(8,128)(2,1)S(1)} %get-tuple-element.23), channel_id=1, source_target_pairs={{0,3},{1,2},{2,1},{3,0},{16,18},{17,19},{18,16},{19,17},{4,7},{5,6... | collective-permute-start | bytes 1179656 | tf_op jit(solution)/shard_map/ppermute | solution.py:38
  32.0 18.6 %copy-start = (bf16[128,128,128]{2,1,0:T(8,128)(2,1)S(1)}, bf16[128,128,128]{2,1,0:T(8,128)(2,1)}, u32[]{:S(2)}) copy-start(bf16[128,128,128]{2,1,0:T(8,128)(2,1)} %refs_0_.1) | copy-start | bytes 12582916
  32.0 18.6 %collective-permute-start.15 = (bf16[11,128,128]{2,1,0:T(8,128)(2,1)S(1)}, bf16[11,128,128]{2,1,0:T(8,128)(2,1)S(1)}, u32[]{:S(2)}, u32[]{:S(2)}) collective-permute-start(bf16[11,128,128]{2,1,0:T(8,128)(2,1)S(1)} %collective-permute-done.refs_3_), channel_id=1, source_target_pairs={{0,16},{16,0},{1,17},{17,1},{2,18},{18,2},{3,19},{19,3},{4,20},{20... | collective-permute-start | bytes 1081352 | tf_op jit(solution)/shard_map/ppermute | solution.py:38
  35.6 8.7 %collective-permute-start.12 = (bf16[9,128,128]{2,1,0:T(8,128)(2,1)S(1)}, bf16[9,128,128]{2,1,0:T(8,128)(2,1)S(1)}, u32[]{:S(2)}, u32[]{:S(2)}) collective-permute-start(bf16[9,128,128]{2,1,0:T(8,128)(2,1)S(1)} %collective-permute-done.11.refs_1_), channel_id=1, source_target_pairs={{0,4},{4,0},{8,12},{12,8},{1,5},{5,1},{9,13},{13,9},{2,6},{6,2},{1... | collective-permute-start | bytes 884744 | tf_op jit(solution)/shard_map/ppermute | solution.py:38
  35.6 15.0 %collective-permute-start.14 = (bf16[9,128,128]{2,1,0:T(8,128)(2,1)S(1)}, bf16[9,128,128]{2,1,0:T(8,128)(2,1)S(1)}, u32[]{:S(2)}, u32[]{:S(2)}) collective-permute-start(bf16[9,128,128]{2,1,0:T(8,128)(2,1)S(1)} %collective-permute-done.11.refs_1_), channel_id=1, source_target_pairs={{0,16},{16,0},{1,17},{17,1},{2,18},{18,2},{3,19},{19,3},{4,20},{20... | collective-permute-start | bytes 884744 | tf_op jit(solution)/shard_map/ppermute | solution.py:38
where the time goes:
time: 53 us; the launch traced here: 52.8 us
  waiting for transfers between devices  29 us (55%)
  starting transfers between devices  14.7 us (28%)
  Pallas kernels  8.1 us (15%)
  local copies, waits for them, and re-layouts  0.93 us (2%)
    ppermute x18, waiting for transfers between devices, hop(): return lax.ppermute(array, axes, pairs)  29 us
    ppermute x18, starting transfers between devices, hop(): return lax.ppermute(array, axes, pairs)  14.7 us
    pallas_call x2, Pallas kernels, cut(): pl.pallas_call(kernel, out_shape=[jax.ShapeDtypeStruct((sum((heads for _,...  2.61 us
    pallas_call x1, Pallas kernels, attend(): pl.pallas_call(kernel, out_shape=jax.ShapeDtypeStruct((heads, spans, per_...  2.5 us
    pallas_call x1, Pallas kernels, project(): pl.pallas_call(kernel, out_shape=jax.ShapeDtypeStruct((spans, per_span, h...  2.21 us
  transfers between devices with their start and end apart: 18, of which 7 were waited for; matrix products, arithmetic and copies ran while one was open for 2% of the time, Pallas kernels for 8%

commit v1 on v0

--- a/solution.py
+++ b/solution.py
@@ -112,8 +112,8 @@
 
 def weight_pieces(value_up, heads, query):
     groups, ctx, wide, subs = (lax.axis_size(name) for name in AXES)
-    pieces = [value_up]
-    rules = [lambda g, c, w, s: [((w * subs + s) * heads, w * subs + s, 0, heads)]]
+    pieces = list(cut(value_up, [[(lambda g, c, w, s: (w * subs + s) * heads, heads)]]))
+    rules = [lambda g, c, w, s: [(0, w * subs + s, 0, heads)]]
     square = groups == 2 and subs == 2 and ctx % 2 == 0
     one, two = heads * PARTS[0] // 32, heads * PARTS[1] // 32
     last = 2 * one + two
@@ -359,7 +359,7 @@
     return pl.pallas_call(
         kernel,
         out_shape=jax.ShapeDtypeStruct((spans, per_span, heads, values), jnp.bfloat16),
-        in_specs=[VMEM, HBM] + [ANY] * (parts - 1),
+        in_specs=[VMEM] + [ANY] * parts,
         out_specs=ANY,
         scratch_shapes=[
             pltpu.VMEM((heads, LAT, values), jnp.bfloat16),

time: 53 us -> 52.9 us (level)
  waiting for transfers between devices: 29 us -> 27.7 us
  Pallas kernels: 8.1 us -> 9.29 us
    ppermute x18, waiting for transfers between devices: 29 us -> 27.7 us  [hop(): return lax.ppermute(array, axes, pairs)]
    pallas_call x2 -> x3, Pallas kernels: 2.61 us -> 3.85 us  [cut(): pl.pallas_call(kernel, out_shape=[jax.ShapeDtypeStruct((sum((heads for _,...]
  transfers between devices with their start and end apart: 18 -> 18, of which waited for: 7 -> 7; matrix products, arithmetic and copies ran while one was open for 2% -> 2% of each run, Pallas kernels for 8% -> 10%
where the time goes in v1:
time: 52.9 us; the launch traced here: 52.7 us
  waiting for transfers between devices  27.7 us (52%)
  starting transfers between devices  14.7 us (28%)
  Pallas kernels  9.29 us (18%)
  local copies, waits for them, and re-layouts  0.9 us (2%)
    ppermute x18, waiting for transfers between devices, hop(): return lax.ppermute(array, axes, pairs)  27.7 us
    ppermute x18, starting transfers between devices, hop(): return lax.ppermute(array, axes, pairs)  14.7 us
    pallas_call x3, Pallas kernels, cut(): pl.pallas_call(kernel, out_shape=[jax.ShapeDtypeStruct((sum((heads for _,...  3.85 us
    pallas_call x1, Pallas kernels, attend(): pl.pallas_call(kernel, out_shape=jax.ShapeDtypeStruct((heads, spans, per_...  2.55 us
    pallas_call x1, Pallas kernels, project(): pl.pallas_call(kernel, out_shape=jax.ShapeDtypeStruct((spans, per_span, h...  2.12 us
  transfers between devices with their start and end apart: 18, of which 7 were waited for; matrix products, arithmetic and copies ran while one was open for 2% of the time, Pallas kernels for 10%

profile of v1, /device:TPU:0, one launch (start us, length us, event | category | flops | bytes accessed | tf_op | source)
XLA Modules:
  0.0 52.7 jit_solution(10622944316060297158)
XLA Ops:
  0.0 1.6 %cut.3 = (bf16[11,128,128]{2,1,0:T(8,128)(2,1)S(1)}, bf16[3,128,128]{2,1,0:T(8,128)(2,1)S(1)}, bf16[12,128,128]{2,1,0:T(8,128)(2,1)S(1)}, bf16[32,128,128]{2,1,0:T(8,128)(2,1)S(1)}) custom-call(bf16[128,128,128]{2,1,0:T(8,128)(2,1)} %whole_ref.5), custom_call_target="tpu_custom_call" | custom-call | tf_op jit(solution)/shard_map/cut/pallas_call | solution.py:97
  1.7 0.6 %collective-permute-start.17 = (bf16[32,128,128]{2,1,0:T(8,128)(2,1)S(1)}, bf16[32,128,128]{2,1,0:T(8,128)(2,1)S(1)}, u32[]{:S(2)}, u32[]{:S(2)}) collective-permute-start(bf16[32,128,128]{2,1,0:T(8,128)(2,1)S(1)} %get-tuple-element.24), channel_id=1, source_target_pairs={{0,1},{1,0},{2,3},{3,2},{16,17},{17,16},{18,19},{19,18},{4,5},{5,4... | collective-permute-start | bytes 3145736 | tf_op jit(solution)/shard_map/ppermute | solution.py:38
  2.2 2.6 %collective-permute-start.13 = (bf16[3,128,128]{2,1,0:T(8,128)(2,1)S(1)}, bf16[3,128,128]{2,1,0:T(8,128)(2,1)S(1)}, u32[]{:S(2)}, u32[]{:S(2)}) collective-permute-start(bf16[3,128,128]{2,1,0:T(8,128)(2,1)S(1)} %get-tuple-element.22), channel_id=1, source_target_pairs={{0,2},{1,3},{2,0},{3,1},{16,19},{17,18},{18,17},{19,16},{4,6},{5,7... | collective-permute-start | bytes 294920 | tf_op jit(solution)/shard_map/ppermute | solution.py:38
  4.8 1.6 %collective-permute-start.1 = (s32[2,2,4]{2,1,0:T(2,128)S(1)}, s32[2,2,4]{2,1,0:T(2,128)S(1)}, u32[]{:S(2)}, u32[]{:S(2)}) collective-permute-start(s32[2,2,4]{2,1,0:T(2,128)S(1)} %bitcast.5), channel_id=1, source_target_pairs={{0,4},{4,0},{8,12},{12,8},{1,5},{5,1},{9,13},{13,9},{2,6},{6,2},{1... | collective-permute-start | bytes 200 | tf_op jit(solution)/shard_map/ppermute | solution.py:38
  6.4 2.6 %collective-permute-start.2 = (s32[2,2,4]{2,1,0:T(2,128)S(1)}, s32[2,2,4]{2,1,0:T(2,128)S(1)}, u32[]{:S(2)}, u32[]{:S(2)}) collective-permute-start(s32[2,2,4]{2,1,0:T(2,128)S(1)} %bitcast.6), channel_id=1, source_target_pairs={{0,8},{4,12},{8,0},{12,4},{1,9},{5,13},{9,1},{13,5},{2,10},{6,14},... | collective-permute-start | bytes 200 | tf_op jit(solution)/shard_map/ppermute | solution.py:38
  8.9 0.2 collective-permute-start.3
  9.2 1.7 %collective-permute-done.2.refs_2_ = s32[2,2,4]{2,1,0:T(2,128)S(1)} collective-permute-done((s32[2,2,4]{2,1,0:T(2,128)S(1)}, s32[2,2,4]{2,1,0:T(2,128)S(1)}, u32[]{:S(2)}, u32[]{:S(2)}) %collective-permute-start.2) | collective-permute-done | bytes 96 | tf_op jit(solution)/shard_map/ppermute | solution.py:38
  10.8 3.6 %collective-permute-done.3.refs_3_ = s32[2,2,4]{2,1,0:T(2,128)S(1)} collective-permute-done((s32[2,2,4]{2,1,0:T(2,128)S(1)}, s32[2,2,4]{2,1,0:T(2,128)S(1)}, u32[]{:S(2)}, u32[]{:S(2)}) %collective-permute-start.3) | collective-permute-done | bytes 96 | tf_op jit(solution)/shard_map/ppermute | solution.py:38
  14.4 0.8 %pick.1 = (bf16[64,1152]{1,0:T(8,128)(2,1)S(1)}, bf16[64,1152]{1,0:T(8,128)(2,1)S(1)}, bf16[64,1152]{1,0:T(8,128)(2,1)S(1)}, bf16[64,1152]{1,0:T(8,128)(2,1)S(1)}) custom-call(s32[2,2,4]{2,1,0:T(2,128)S(1)} %bitcast.8, s32[2,2,4]{2,1,0:T(2,128)S(1)} %collective-permute-done.1.refs_1_, s32[2,2,4]{2,1,0:T(2,128)S(1)} %collective-permute-done.2.refs_2_, ...), custom_call_target="tpu_custom_call" | custom-call | tf_op jit(solution)/shard_map/pick/pallas_call | solution.py:64
  15.2 0.2 collective-permute-start.6
  15.4 0.5 collective-permute-start
  15.9 0.0 collective-permute-start.4
  15.9 1.0 %cut.5 = bf16[9,128,128]{2,1,0:T(8,128)(2,1)S(1)} custom-call(bf16[128,128,128]{2,1,0:T(8,128)(2,1)} %whole_ref.5), custom_call_target="tpu_custom_call" | custom-call | tf_op jit(solution)/shard_map/cut/pallas_call | solution.py:97
  16.9 1.6 %collective-permute-start.11 = (bf16[9,128,128]{2,1,0:T(8,128)(2,1)S(1)}, bf16[9,128,128]{2,1,0:T(8,128)(2,1)S(1)}, u32[]{:S(2)}, u32[]{:S(2)}) collective-permute-start(bf16[9,128,128]{2,1,0:T(8,128)(2,1)S(1)} %cut.5), channel_id=1, source_target_pairs={{0,2},{1,3},{2,0},{3,1},{16,19},{17,18},{18,17},{19,16},{4,6},{5,7... | collective-permute-start | bytes 884744 | tf_op jit(solution)/shard_map/ppermute | solution.py:38
  18.5 5.4 %collective-permute-done.6.refs_3_ = bf16[64,1152]{1,0:T(8,128)(2,1)S(1)} collective-permute-done((bf16[64,1152]{1,0:T(8,128)(2,1)S(1)}, bf16[64,1152]{1,0:T(8,128)(2,1)S(1)}, u32[]{:S(2)}, u32[]{:S(2)}) %collective-permute-start.6) | collective-permute-done | bytes 147488 | tf_op jit(solution)/shard_map/ppermute | solution.py:38
  23.9 6.0 %collective-permute-done.5.refs_2_ = bf16[64,1152]{1,0:T(8,128)(2,1)S(1)} collective-permute-done((bf16[64,1152]{1,0:T(8,128)(2,1)S(1)}, bf16[64,1152]{1,0:T(8,128)(2,1)S(1)}, u32[]{:S(2)}, u32[]{:S(2)}) %collective-permute-start.5) | collective-permute-done | bytes 147488 | tf_op jit(solution)/shard_map/ppermute | solution.py:38
  29.9 0.0 collective-permute-start.10
  29.9 0.0 collective-permute-done.7.refs_4_
  29.9 0.5 collective-permute-start.8
  30.4 0.0 collective-permute-done.11.refs_1_
  30.4 0.1 collective-permute-start.9
  30.5 0.0 collective-permute-done.refs_3_
  30.5 0.6 %collective-permute-start.16 = (bf16[12,128,128]{2,1,0:T(8,128)(2,1)S(1)}, bf16[12,128,128]{2,1,0:T(8,128)(2,1)S(1)}, u32[]{:S(2)}, u32[]{:S(2)}) collective-permute-start(bf16[12,128,128]{2,1,0:T(8,128)(2,1)S(1)} %get-tuple-element.23), channel_id=1, source_target_pairs={{0,3},{1,2},{2,1},{3,0},{16,18},{17,19},{18,16},{19,17},{4,7},{5,6... | collective-permute-start | bytes 1179656 | tf_op jit(solution)/shard_map/ppermute | solution.py:38
  31.1 0.9 %copy.7 = bf16[2,32,32,576]{3,1,2,0:T(8,128)(2,1)S(1)} copy(bf16[2,32,32,576]{3,2,1,0:T(8,128)(2,1)S(1)} %copy-done.2) | data formatting | bytes 4718592 | tf_op args[0]
  32.0 3.6 %collective-permute-start.15 = (bf16[11,128,128]{2,1,0:T(8,128)(2,1)S(1)}, bf16[11,128,128]{2,1,0:T(8,128)(2,1)S(1)}, u32[]{:S(2)}, u32[]{:S(2)}) collective-permute-start(bf16[11,128,128]{2,1,0:T(8,128)(2,1)S(1)} %collective-permute-done.refs_3_), channel_id=1, source_target_pairs={{0,16},{16,0},{1,17},{17,1},{2,18},{18,2},{3,19},{19,3},{4,20},{20... | collective-permute-start | bytes 1081352 | tf_op jit(solution)/shard_map/ppermute | solution.py:38
  35.6 0.2 collective-permute-start.14
  35.7 1.2 %cut.4.refs_0_ = bf16[32,128,128]{2,1,0:T(8,128)(2,1)S(1)} custom-call(bf16[128,128,128]{2,1,0:T(8,128)(2,1)} %whole_ref.5), custom_call_target="tpu_custom_call" | custom-call | tf_op jit(solution)/shard_map/cut/pallas_call | solution.py:97
  37.0 2.6 %attend.1.latent_ref = bf16[32,2,32,512]{3,2,1,0:T(8,128)(2,1)S(1)} custom-call(s32[2,2,4]{2,1,0:T(2,128)S(1)} %bitcast.9, bf16[2,32,32,576]{3,2,1,0:T(8,128)(2,1)S(1)} %bitcast.4, bf16[64,1152]{1,0:T(8,128)(2,1)S(1)} %get-tuple-element.17.refs_0_, bf16[64,1152]{1,0:T(8,128)(2,1)S(1)} %collective-permute-done.4.refs_1_, ...), custom_call_target="tpu_custom_call" | custom-call | tf_op jit(solution)/shard_map/attend/pallas_call | solution.py:282
  39.5 1.8 %collective-permute-done.16.refs_7_ = bf16[12,128,128]{2,1,0:T(8,128)(2,1)S(1)} collective-permute-done((bf16[12,128,128]{2,1,0:T(8,128)(2,1)S(1)}, bf16[12,128,128]{2,1,0:T(8,128)(2,1)S(1)}, u32[]{:S(2)}, u32[]{:S(2)}) %collective-permute-start.16) | collective-permute-done | bytes 393248 | tf_op jit(solution)/shard_map/ppermute | solution.py:38
  41.3 3.0 %collective-permute-done.12.refs_2_ = bf16[9,128,128]{2,1,0:T(8,128)(2,1)S(1)} collective-permute-done((bf16[9,128,128]{2,1,0:T(8,128)(2,1)S(1)}, bf16[9,128,128]{2,1,0:T(8,128)(2,1)S(1)}, u32[]{:S(2)}, u32[]{:S(2)}) %collective-permute-start.12) | collective-permute-done | bytes 294944 | tf_op jit(solution)/shard_map/ppermute | solution.py:38
  44.3 6.3 %collective-permute-done.14.refs_5_ = bf16[9,128,128]{2,1,0:T(8,128)(2,1)S(1)} collective-permute-done((bf16[9,128,128]{2,1,0:T(8,128)(2,1)S(1)}, bf16[9,128,128]{2,1,0:T(8,128)(2,1)S(1)}, u32[]{:S(2)}, u32[]{:S(2)}) %collective-permute-start.14) | collective-permute-done | bytes 294944 | tf_op jit(solution)/shard_map/ppermute | solution.py:38
  50.6 2.1 %project.1 = bf16[2,32,32,128]{3,2,1,0:T(8,128)(2,1)} custom-call(bf16[32,2,32,512]{3,2,1,0:T(8,128)(2,1)S(1)} %attend.1.latent_ref, bf16[32,128,128]{2,1,0:T(8,128)(2,1)S(1)} %cut.4.refs_0_, bf16[9,128,128]{2,1,0:T(8,128)(2,1)S(1)} %collective-permute-done.11.refs_1_, bf16[9,128,128]{2,1,0:T(8,128)(2,1)S(1)} %collective-permute-done.12.refs_2_, ...), custom_call_target="tpu_custom_call" | custom-call | tf_op jit(solution)/shard_map/project/pallas_call | solution.py:359
  (17 shorter events, 0.0 us)
Async XLA Ops:
  0.0 4.8 %copy-start.1 = (s32[2,4,2]{1,2,0:T(2,128)S(1)}, s32[2,4,2]{1,2,0:T(2,128)}, u32[]{:S(2)}) copy-start(s32[2,4,2]{1,2,0:T(2,128)} %param.5) | copy-start | bytes 196
  0.0 14.4 %copy-start = (bf16[16,64,576]{2,1,0:T(8,128)(2,1)S(1)}, bf16[16,64,576]{2,1,0:T(8,128)(2,1)}, u32[]{:S(2)}) copy-start(bf16[16,64,576]{2,1,0:T(8,128)(2,1)} %refs_4_.1) | copy-start | bytes 3538948
  1.7 48.9 %collective-permute-start.17 = (bf16[32,128,128]{2,1,0:T(8,128)(2,1)S(1)}, bf16[32,128,128]{2,1,0:T(8,128)(2,1)S(1)}, u32[]{:S(2)}, u32[]{:S(2)}) collective-permute-start(bf16[32,128,128]{2,1,0:T(8,128)(2,1)S(1)} %get-tuple-element.24), channel_id=1, source_target_pairs={{0,1},{1,0},{2,3},{3,2},{16,17},{17,16},{18,19},{19,18},{4,5},{5,4... | collective-permute-start | bytes 3145736 | tf_op jit(solution)/shard_map/ppermute | solution.py:38
  2.2 14.7 %collective-permute-start.13 = (bf16[3,128,128]{2,1,0:T(8,128)(2,1)S(1)}, bf16[3,128,128]{2,1,0:T(8,128)(2,1)S(1)}, u32[]{:S(2)}, u32[]{:S(2)}) collective-permute-start(bf16[3,128,128]{2,1,0:T(8,128)(2,1)S(1)} %get-tuple-element.22), channel_id=1, source_target_pairs={{0,2},{1,3},{2,0},{3,1},{16,19},{17,18},{18,17},{19,16},{4,6},{5,7... | collective-permute-start | bytes 294920 | tf_op jit(solution)/shard_map/ppermute | solution.py:38
  4.8 26.3 %copy-start.2 = (bf16[2,32,32,576]{3,2,1,0:T(8,128)(2,1)S(1)}, bf16[2,32,32,576]{3,2,1,0:T(8,128)(2,1)}, u32[]{:S(2)}) copy-start(bf16[2,32,32,576]{3,2,1,0:T(8,128)(2,1)} %param.4) | copy-start | bytes 7077892
  4.8 4.4 %collective-permute-start.1 = (s32[2,2,4]{2,1,0:T(2,128)S(1)}, s32[2,2,4]{2,1,0:T(2,128)S(1)}, u32[]{:S(2)}, u32[]{:S(2)}) collective-permute-start(s32[2,2,4]{2,1,0:T(2,128)S(1)} %bitcast.5), channel_id=1, source_target_pairs={{0,4},{4,0},{8,12},{12,8},{1,5},{5,1},{9,13},{13,9},{2,6},{6,2},{1... | collective-permute-start | bytes 200 | tf_op jit(solution)/shard_map/ppermute | solution.py:38
  6.4 4.5 %collective-permute-start.2 = (s32[2,2,4]{2,1,0:T(2,128)S(1)}, s32[2,2,4]{2,1,0:T(2,128)S(1)}, u32[]{:S(2)}, u32[]{:S(2)}) collective-permute-start(s32[2,2,4]{2,1,0:T(2,128)S(1)} %bitcast.6), channel_id=1, source_target_pairs={{0,8},{4,12},{8,0},{12,4},{1,9},{5,13},{9,1},{13,5},{2,10},{6,14},... | collective-permute-start | bytes 200 | tf_op jit(solution)/shard_map/ppermute | solution.py:38
  8.9 5.5 %collective-permute-start.3 = (s32[2,2,4]{2,1,0:T(2,128)S(1)}, s32[2,2,4]{2,1,0:T(2,128)S(1)}, u32[]{:S(2)}, u32[]{:S(2)}) collective-permute-start(s32[2,2,4]{2,1,0:T(2,128)S(1)} %bitcast.7), channel_id=1, source_target_pairs={{0,12},{4,8},{8,4},{12,0},{1,13},{5,9},{9,5},{13,1},{2,14},{6,10},... | collective-permute-start | bytes 200 | tf_op jit(solution)/shard_map/ppermute | solution.py:38
  15.2 8.7 %collective-permute-start.6 = (bf16[64,1152]{1,0:T(8,128)(2,1)S(1)}, bf16[64,1152]{1,0:T(8,128)(2,1)S(1)}, u32[]{:S(2)}, u32[]{:S(2)}) collective-permute-start(bf16[64,1152]{1,0:T(8,128)(2,1)S(1)} %get-tuple-element.20), channel_id=1, source_target_pairs={{0,12},{4,8},{8,4},{12,0},{1,13},{5,9},{9,5},{13,1},{2,14},{6,10},... | collective-permute-start | bytes 442376 | tf_op jit(solution)/shard_map/ppermute | solution.py:38
  15.4 15.1 %collective-permute-start = (bf16[11,128,128]{2,1,0:T(8,128)(2,1)S(1)}, bf16[11,128,128]{2,1,0:T(8,128)(2,1)S(1)}, u32[]{:S(2)}, u32[]{:S(2)}) collective-permute-start(bf16[11,128,128]{2,1,0:T(8,128)(2,1)S(1)} %get-tuple-element.15), channel_id=1, source_target_pairs={{0,2},{1,3},{2,0},{3,1},{16,19},{17,18},{18,17},{19,16},{4,6},{5,7... | collective-permute-start | bytes 1081352 | tf_op jit(solution)/shard_map/ppermute | solution.py:38
  15.9 8.0 %collective-permute-start.4 = (bf16[64,1152]{1,0:T(8,128)(2,1)S(1)}, bf16[64,1152]{1,0:T(8,128)(2,1)S(1)}, u32[]{:S(2)}, u32[]{:S(2)}) collective-permute-start(bf16[64,1152]{1,0:T(8,128)(2,1)S(1)} %get-tuple-element.18), channel_id=1, source_target_pairs={{0,4},{4,0},{8,12},{12,8},{1,5},{5,1},{9,13},{13,9},{2,6},{6,2},{1... | collective-permute-start | bytes 442376 | tf_op jit(solution)/shard_map/ppermute | solution.py:38
  16.9 13.6 %collective-permute-start.11 = (bf16[9,128,128]{2,1,0:T(8,128)(2,1)S(1)}, bf16[9,128,128]{2,1,0:T(8,128)(2,1)S(1)}, u32[]{:S(2)}, u32[]{:S(2)}) collective-permute-start(bf16[9,128,128]{2,1,0:T(8,128)(2,1)S(1)} %cut.5), channel_id=1, source_target_pairs={{0,2},{1,3},{2,0},{3,1},{16,19},{17,18},{18,17},{19,16},{4,6},{5,7... | collective-permute-start | bytes 884744 | tf_op jit(solution)/shard_map/ppermute | solution.py:38
  23.9 6.0 %collective-permute-start.5 = (bf16[64,1152]{1,0:T(8,128)(2,1)S(1)}, bf16[64,1152]{1,0:T(8,128)(2,1)S(1)}, u32[]{:S(2)}, u32[]{:S(2)}) collective-permute-start(bf16[64,1152]{1,0:T(8,128)(2,1)S(1)} %get-tuple-element.19), channel_id=1, source_target_pairs={{0,8},{4,12},{8,0},{12,4},{1,9},{5,13},{9,1},{13,5},{2,10},{6,14},... | collective-permute-start | bytes 442376 | tf_op jit(solution)/shard_map/ppermute | solution.py:38
  23.9 6.0 %collective-permute-start.7 = (bf16[64,1152]{1,0:T(8,128)(2,1)S(1)}, bf16[64,1152]{1,0:T(8,128)(2,1)S(1)}, u32[]{:S(2)}, u32[]{:S(2)}) collective-permute-start(bf16[64,1152]{1,0:T(8,128)(2,1)S(1)} %get-tuple-element.17.refs_0_), channel_id=1, source_target_pairs={{0,1},{1,0},{2,3},{3,2},{4,5},{5,4},{6,7},{7,6},{8,9},{9,8},{10,11... | collective-permute-start | bytes 442376 | tf_op jit(solution)/shard_map/ppermute | solution.py:38
  29.9 2.1 %collective-permute-start.10 = (bf16[64,1152]{1,0:T(8,128)(2,1)S(1)}, bf16[64,1152]{1,0:T(8,128)(2,1)S(1)}, u32[]{:S(2)}, u32[]{:S(2)}) collective-permute-start(bf16[64,1152]{1,0:T(8,128)(2,1)S(1)} %collective-permute-done.6.refs_3_), channel_id=1, source_target_pairs={{0,1},{1,0},{2,3},{3,2},{4,5},{5,4},{6,7},{7,6},{8,9},{9,8},{10,11... | collective-permute-start | bytes 442376 | tf_op jit(solution)/shard_map/ppermute | solution.py:38
  29.9 5.6 %collective-permute-start.8 = (bf16[64,1152]{1,0:T(8,128)(2,1)S(1)}, bf16[64,1152]{1,0:T(8,128)(2,1)S(1)}, u32[]{:S(2)}, u32[]{:S(2)}) collective-permute-start(bf16[64,1152]{1,0:T(8,128)(2,1)S(1)} %collective-permute-done.4.refs_1_), channel_id=1, source_target_pairs={{0,1},{1,0},{2,3},{3,2},{4,5},{5,4},{6,7},{7,6},{8,9},{9,8},{10,11... | collective-permute-start | bytes 442376 | tf_op jit(solution)/shard_map/ppermute | solution.py:38
  30.4 5.1 %collective-permute-start.9 = (bf16[64,1152]{1,0:T(8,128)(2,1)S(1)}, bf16[64,1152]{1,0:T(8,128)(2,1)S(1)}, u32[]{:S(2)}, u32[]{:S(2)}) collective-permute-start(bf16[64,1152]{1,0:T(8,128)(2,1)S(1)} %collective-permute-done.5.refs_2_), channel_id=1, source_target_pairs={{0,1},{1,0},{2,3},{3,2},{4,5},{5,4},{6,7},{7,6},{8,9},{9,8},{10,11... | collective-permute-start | bytes 442376 | tf_op jit(solution)/shard_map/ppermute | solution.py:38
  30.5 10.8 %collective-permute-start.16 = (bf16[12,128,128]{2,1,0:T(8,128)(2,1)S(1)}, bf16[12,128,128]{2,1,0:T(8,128)(2,1)S(1)}, u32[]{:S(2)}, u32[]{:S(2)}) collective-permute-start(bf16[12,128,128]{2,1,0:T(8,128)(2,1)S(1)} %get-tuple-element.23), channel_id=1, source_target_pairs={{0,3},{1,2},{2,1},{3,0},{16,18},{17,19},{18,16},{19,17},{4,7},{5,6... | collective-permute-start | bytes 1179656 | tf_op jit(solution)/shard_map/ppermute | solution.py:38
  32.0 18.6 %collective-permute-start.15 = (bf16[11,128,128]{2,1,0:T(8,128)(2,1)S(1)}, bf16[11,128,128]{2,1,0:T(8,128)(2,1)S(1)}, u32[]{:S(2)}, u32[]{:S(2)}) collective-permute-start(bf16[11,128,128]{2,1,0:T(8,128)(2,1)S(1)} %collective-permute-done.refs_3_), channel_id=1, source_target_pairs={{0,16},{16,0},{1,17},{17,1},{2,18},{18,2},{3,19},{19,3},{4,20},{20... | collective-permute-start | bytes 1081352 | tf_op jit(solution)/shard_map/ppermute | solution.py:38
  35.6 8.7 %collective-permute-start.12 = (bf16[9,128,128]{2,1,0:T(8,128)(2,1)S(1)}, bf16[9,128,128]{2,1,0:T(8,128)(2,1)S(1)}, u32[]{:S(2)}, u32[]{:S(2)}) collective-permute-start(bf16[9,128,128]{2,1,0:T(8,128)(2,1)S(1)} %collective-permute-done.11.refs_1_), channel_id=1, source_target_pairs={{0,4},{4,0},{8,12},{12,8},{1,5},{5,1},{9,13},{13,9},{2,6},{6,2},{1... | collective-permute-start | bytes 884744 | tf_op jit(solution)/shard_map/ppermute | solution.py:38
  35.6 15.0 %collective-permute-start.14 = (bf16[9,128,128]{2,1,0:T(8,128)(2,1)S(1)}, bf16[9,128,128]{2,1,0:T(8,128)(2,1)S(1)}, u32[]{:S(2)}, u32[]{:S(2)}) collective-permute-start(bf16[9,128,128]{2,1,0:T(8,128)(2,1)S(1)} %collective-permute-done.11.refs_1_), channel_id=1, source_target_pairs={{0,16},{16,0},{1,17},{17,1},{2,18},{18,2},{3,19},{19,3},{4,20},{20... | collective-permute-start | bytes 884744 | tf_op jit(solution)/shard_map/ppermute | solution.py:38
